TPU v7x, 128 devices: a whole 4x4x4 slice. The times are simulated.
128 devices in a mesh: dp: 8 (over z_lo, x), seq: 16 (over z_hi, y, core).
Axes of the slice: x: 4, y: 4, z: 4 (z_hi: 2, z_lo: 2; z = z_hi * 2 + z_lo), core: 2. Of those that a mesh axis runs over, the one named last changes fastest.
Arguments:
- series: bfloat16 [8, 8192, 128], P('dp', 'seq'), may hold values from -6 to 6
- cotangent: bfloat16 [8, 8192, 128], P('dp', 'seq'), may hold values from -6 to 6
- w_in: bfloat16 [128, 384], replicated, may hold values from -0.5 to 0.5
- w_out: bfloat16 [128, 128], replicated, may hold values from -0.5 to 0.5
- taps: float32 [3, 384], replicated, may hold values from -3 to 3
- skip_one: float32 [128], replicated, may hold values from 0.5 to 1.5
- skip_two: float32 [128], replicated, may hold values from 0.5 to 1.5
- filter_one: float32 [8, 8192], P(None, 'seq'), may hold values from -0.0625 to 0.0625
- filter_two: float32 [8, 8192], P(None, 'seq'), may hold values from -0.0625 to 0.0625
Outputs:
- output: bfloat16 [8, 8192, 128], P('dp', 'seq')
- d_series: bfloat16 [8, 8192, 128], P('dp', 'seq')
- grad_w_in: float32 [128, 384], replicated
- grad_w_out: float32 [128, 128], replicated
- grad_taps: float32 [3, 384], replicated
- grad_skip_one: float32 [128], replicated
- grad_skip_two: float32 [128], replicated
- grad_filter_one: float32 [8, 8192], P(None, 'seq')
- grad_filter_two: float32 [8, 8192], P(None, 'seq')
All inputs are finite; a program needn't handle non-finite values.
Results may differ from a plain program's by a relative error of at most 0.015.
Values may be sent and summed in bfloat16 or wider, within the bound.
A program may use at most 128 MiB of HBM per device.

v0:
```python
import math
import jax
import jax.numpy as jnp
from jax import lax
from jax.sharding import PartitionSpec as P

FACTOR = 32


def passed_along(block, axis, distance):
    devices = range(lax.axis_size(axis))
    route = [(i - distance, i) for i in devices if i - distance in devices]
    return lax.ppermute(block, axis, route)


def grid_index(shape_pair, along):
    return lax.broadcasted_iota(jnp.int32, shape_pair, along)


def twiddle(row_index, col_index, period, direction):
    angle = (
        direction * 2.0 * math.pi / period * (row_index * col_index % period).astype(jnp.float32)
    )
    return (jnp.cos(angle), jnp.sin(angle))


def complex_mul(left_real, left_imag, right_real, right_imag):
    return (
        left_real * right_real - left_imag * right_imag,
        left_real * right_imag + left_imag * right_real,
    )


def complex_dft(real_part, imag_part, table_real, table_imag, pattern):
    highest = lax.Precision.HIGHEST
    first = jnp.einsum(pattern, table_real, real_part, precision=highest)
    second = jnp.einsum(pattern, table_imag, imag_part, precision=highest)
    third = jnp.einsum(pattern, table_real, imag_part, precision=highest)
    fourth = jnp.einsum(pattern, table_imag, real_part, precision=highest)
    return (first - second, third + fourth)


def local_dft(pieces):
    real_part, imag_part = pieces
    series_count, pair_rows, block_rows, channels = real_part.shape
    inner = block_rows // FACTOR
    real_part = real_part.reshape(series_count, pair_rows, FACTOR, inner, channels)
    imag_part = imag_part.reshape(series_count, pair_rows, FACTOR, inner, channels)
    table_real, table_imag = twiddle(
        grid_index((FACTOR, FACTOR), 0), grid_index((FACTOR, FACTOR), 1), FACTOR, -1.0
    )
    real_part, imag_part = complex_dft(
        real_part, imag_part, table_real, table_imag, "ca,erabk->ercbk"
    )
    turn_real, turn_imag = twiddle(
        grid_index((FACTOR, inner), 0), grid_index((FACTOR, inner), 1), block_rows, -1.0
    )
    real_part, imag_part = complex_mul(
        real_part, imag_part, turn_real[:, :, None], turn_imag[:, :, None]
    )
    table_real, table_imag = twiddle(
        grid_index((inner, inner), 0), grid_index((inner, inner), 1), inner, -1.0
    )
    return complex_dft(real_part, imag_part, table_real, table_imag, "db,ercbk->ercdk")


def local_inverse(real_part, imag_part):
    series_count, pair_rows, outer, inner, channels = real_part.shape
    block_rows = outer * inner
    table_real, table_imag = twiddle(
        grid_index((inner, inner), 0), grid_index((inner, inner), 1), inner, 1.0
    )
    real_part, imag_part = complex_dft(
        real_part, imag_part, table_real, table_imag, "bd,ercdk->ercbk"
    )
    turn_real, turn_imag = twiddle(
        grid_index((outer, inner), 0), grid_index((outer, inner), 1), block_rows, 1.0
    )
    real_part, imag_part = complex_mul(
        real_part, imag_part, turn_real[:, :, None], turn_imag[:, :, None]
    )
    table_real, table_imag = twiddle(
        grid_index((outer, outer), 0), grid_index((outer, outer), 1), outer, 1.0
    )
    real_part, imag_part = complex_dft(
        real_part, imag_part, table_real, table_imag, "ac,ercbk->erabk"
    )
    return (
        real_part.reshape(series_count, pair_rows, block_rows, channels),
        imag_part.reshape(series_count, pair_rows, block_rows, channels),
    )


def first_section(columns):
    highest = lax.Precision.HIGHEST
    groups = lax.axis_size("seq")
    column_width = columns.shape[2]
    period = 2 * groups * groups * column_width
    offset = lax.axis_index("seq") * column_width
    table_real, table_imag = twiddle(
        grid_index((2 * groups, groups), 0), grid_index((2 * groups, groups), 1), 2 * groups, -1.0
    )
    real_part = jnp.einsum("kn,enjc->ekjc", table_real, columns, precision=highest)
    imag_part = jnp.einsum("kn,enjc->ekjc", table_imag, columns, precision=highest)
    turn_real, turn_imag = twiddle(
        grid_index((2 * groups, column_width), 0),
        grid_index((2 * groups, column_width), 1) + offset,
        period,
        -1.0,
    )
    return complex_mul(real_part, imag_part, turn_real[:, :, None], turn_imag[:, :, None])


def last_section(pieces):
    highest = lax.Precision.HIGHEST
    part_real, part_imag = pieces
    groups = lax.axis_size("seq")
    column_width = part_real.shape[2]
    period = 2 * groups * groups * column_width
    offset = lax.axis_index("seq") * column_width
    turn_real, turn_imag = twiddle(
        grid_index((2 * groups, column_width), 0),
        grid_index((2 * groups, column_width), 1) + offset,
        period,
        1.0,
    )
    part_real, part_imag = complex_mul(
        part_real, part_imag, turn_real[:, :, None], turn_imag[:, :, None]
    )
    table_real, table_imag = twiddle(
        grid_index((groups, 2 * groups), 0), grid_index((groups, 2 * groups), 1), 2 * groups, 1.0
    )
    summed = jnp.einsum("nk,ekjc->enjc", table_real, part_real, precision=highest) - jnp.einsum(
        "nk,ekjc->enjc", table_imag, part_imag, precision=highest
    )
    return summed * (1.0 / period)


def to_frequency(real_part, imag_part):
    return local_dft(
        (
            lax.all_to_all(real_part, "seq", split_axis=1, concat_axis=2, tiled=True),
            lax.all_to_all(imag_part, "seq", split_axis=1, concat_axis=2, tiled=True),
        )
    )


def spectrum(field):
    real_part, imag_part = first_section(
        lax.all_to_all(field, "seq", split_axis=2, concat_axis=1, tiled=True)
    )
    return to_frequency(real_part, imag_part)


def signal(real_part, imag_part):
    real_part, imag_part = local_inverse(real_part, imag_part)
    columns = last_section(
        (
            lax.all_to_all(real_part, "seq", split_axis=2, concat_axis=1, tiled=True),
            lax.all_to_all(imag_part, "seq", split_axis=2, concat_axis=1, tiled=True),
        )
    )
    return lax.all_to_all(columns, "seq", split_axis=1, concat_axis=2, tiled=True)


def order_spectrum(real_part, imag_part):
    series_count, pair_rows, outer, inner, channels = real_part.shape
    block_rows = outer * inner
    real_part = jnp.swapaxes(real_part, 2, 3).reshape(series_count, pair_rows, block_rows, channels)
    imag_part = jnp.swapaxes(imag_part, 2, 3).reshape(series_count, pair_rows, block_rows, channels)
    real_part, imag_part = (
        lax.all_to_all(real_part, "seq", split_axis=2, concat_axis=1, tiled=True),
        lax.all_to_all(imag_part, "seq", split_axis=2, concat_axis=1, tiled=True),
    )
    return (jnp.swapaxes(real_part, 1, 2), jnp.swapaxes(imag_part, 1, 2))


def restore_spectrum(real_part, imag_part):
    real_part = jnp.swapaxes(real_part, 1, 2)
    imag_part = jnp.swapaxes(imag_part, 1, 2)
    real_part, imag_part = (
        lax.all_to_all(real_part, "seq", split_axis=1, concat_axis=2, tiled=True),
        lax.all_to_all(imag_part, "seq", split_axis=1, concat_axis=2, tiled=True),
    )
    series_count, pair_rows, block_rows, channels = real_part.shape
    inner = block_rows // FACTOR
    real_part = jnp.swapaxes(
        real_part.reshape(series_count, pair_rows, inner, FACTOR, channels), 2, 3
    )
    imag_part = jnp.swapaxes(
        imag_part.reshape(series_count, pair_rows, inner, FACTOR, channels), 2, 3
    )
    return (real_part, imag_part)


def transform(field):
    real_part, imag_part = spectrum(field)
    real_part, imag_part = order_spectrum(real_part, imag_part)
    return (real_part, imag_part)


def untransform(real_part, imag_part, in_columns):
    real_part, imag_part = restore_spectrum(real_part, imag_part)
    return signal(real_part, imag_part)


def widen_groups(pieces, channels):
    real_part, imag_part = pieces
    repeat_count = channels // real_part.shape[-1]
    return (
        jnp.repeat(real_part, repeat_count, axis=-1),
        jnp.repeat(imag_part, repeat_count, axis=-1),
    )


def group_sum(pieces, filters):
    result = []
    for piece in pieces:
        channels = piece.shape[-1]
        reshaped = piece.reshape(piece.shape[:-1] + (filters, channels // filters))
        result.append(jnp.sum(jnp.sum(reshaped, axis=-1), axis=0, keepdims=True))
    return (result[0], result[1])


def rows_before(field):
    return passed_along(field[:, :, -2:], "seq", 1)


def rows_after(field):
    return passed_along(field[:, :, :2], "seq", -1)


def filter_blocks(filter_rows):
    return filter_rows.T.reshape(1, 1, filter_rows.shape[1], filter_rows.shape[0])


def shards(series, cotangent, w_in, w_out, taps, skip_one, skip_two, filter_one, filter_two):
    series_count, block_rows, width_d = series.shape
    filters = filter_one.shape[0]
    token_total = series_count * lax.axis_size("dp") * block_rows * lax.axis_size("seq")
    grad_scale = 1.0 / math.sqrt(token_total)
    series_four = series.reshape(series_count, 1, block_rows, width_d)
    cot_four = cotangent.reshape(series_count, 1, block_rows, width_d)
    series_here, cot_here = (series_four, cot_four)
    projected = jnp.einsum("entd,dc->entc", series_here, w_in, preferred_element_type=jnp.float32)
    before = rows_before(projected)
    extended = jnp.concatenate([before, projected], axis=2)
    run_rows = projected.shape[2]
    convolved = (
        taps[0] * extended[:, :, 2:]
        + taps[1] * extended[:, :, 1:-1]
        + taps[2] * extended[:, :, :-2]
    )
    value_part = convolved[..., :width_d]
    gate_one = convolved[..., width_d : 2 * width_d]
    gate_two = convolved[..., 2 * width_d :]
    spec_one = transform(filter_blocks(filter_one))
    spec_two = transform(filter_blocks(filter_two))
    one_real, one_imag = widen_groups(spec_one, width_d)
    two_real, two_imag = widen_groups(spec_two, width_d)
    value_real, value_imag = transform(value_part)
    y_one = (
        untransform(*complex_mul(one_real, one_imag, value_real, value_imag), False)
        + skip_one * value_part
    )
    gated_mid = gate_one * y_one
    mid_real, mid_imag = transform(gated_mid)
    y_two = (
        untransform(*complex_mul(two_real, two_imag, mid_real, mid_imag), False)
        + skip_two * gated_mid
    )
    product = (gate_two * y_two).astype(jnp.bfloat16)
    output = jnp.einsum("entc,cd->entd", product, w_out, preferred_element_type=jnp.float32).astype(
        jnp.bfloat16
    )
    d_product = jnp.einsum("entd,cd->entc", cot_here, w_out, preferred_element_type=jnp.float32)
    grad_two = d_product * gate_two
    d_gate_two = d_product * y_two
    gtwo_real, gtwo_imag = transform(grad_two)
    d_mid = (
        untransform(*complex_mul(two_real, -two_imag, gtwo_real, gtwo_imag), False)
        + skip_two * grad_two
    )
    filter_two_spec = group_sum(complex_mul(mid_real, -mid_imag, gtwo_real, gtwo_imag), filters)
    filter_two_time = untransform(filter_two_spec[0], filter_two_spec[1], False)[0, 0].T
    grad_one = d_mid * gate_one
    d_gate_one = d_mid * y_one
    gone_real, gone_imag = transform(grad_one)
    d_value = (
        untransform(*complex_mul(one_real, -one_imag, gone_real, gone_imag), False)
        + skip_one * grad_one
    )
    filter_one_spec = group_sum(complex_mul(value_real, -value_imag, gone_real, gone_imag), filters)
    filter_one_time = untransform(filter_one_spec[0], filter_one_spec[1], False)[0, 0].T
    d_convolved = jnp.concatenate([d_value, d_gate_one, d_gate_two], axis=3)
    after = rows_after(d_convolved)
    extended_back = jnp.concatenate([d_convolved, after], axis=2)
    d_projected = (
        taps[0] * extended_back[:, :, :-2]
        + taps[1] * extended_back[:, :, 1:-1]
        + taps[2] * extended_back[:, :, 2:]
    ).astype(jnp.bfloat16)
    d_series = jnp.einsum(
        "entc,dc->entd", d_projected, w_in, preferred_element_type=jnp.float32
    ).astype(jnp.bfloat16)
    local_w_in = jnp.einsum(
        "entd,entc->dc", series_here, d_projected, preferred_element_type=jnp.float32
    )
    local_w_out = jnp.einsum("entc,entd->cd", product, cot_here, preferred_element_type=jnp.float32)
    local_taps = jnp.stack(
        [
            jnp.sum(
                d_convolved * extended[:, :, 2 - offset : 2 - offset + run_rows], axis=(0, 1, 2)
            )
            for offset in range(3)
        ]
    )
    local_skip_one = jnp.sum(grad_one * value_part, axis=(0, 1, 2))
    local_skip_two = jnp.sum(grad_two * gated_mid, axis=(0, 1, 2))
    grad_w_in, grad_w_out, grad_taps, grad_skip_one, grad_skip_two = lax.psum(
        (local_w_in, local_w_out, local_taps, local_skip_one, local_skip_two), ("dp", "seq")
    )
    grad_filter_one, grad_filter_two = (
        lax.psum(filter_one_time.astype(jnp.bfloat16), "dp").astype(jnp.float32),
        lax.psum(filter_two_time.astype(jnp.bfloat16), "dp").astype(jnp.float32),
    )
    output = output.reshape(series_count, block_rows, width_d)
    d_series = d_series.reshape(series_count, block_rows, width_d)
    return (
        output,
        d_series,
        grad_scale * grad_w_in,
        grad_scale * grad_w_out,
        grad_scale * grad_taps,
        grad_scale * grad_skip_one,
        grad_scale * grad_skip_two,
        grad_scale * grad_filter_one,
        grad_scale * grad_filter_two,
    )


def solution(mesh):
    in_specs = (
        P("dp", "seq", None),
        P("dp", "seq", None),
        P(),
        P(),
        P(),
        P(),
        P(),
        P(None, "seq"),
        P(None, "seq"),
    )
    out_specs = (
        P("dp", "seq", None),
        P("dp", "seq", None),
        P(),
        P(),
        P(),
        P(),
        P(),
        P(None, "seq"),
        P(None, "seq"),
    )
    return jax.shard_map(shards, mesh=mesh, in_specs=in_specs, out_specs=out_specs, check_vma=False)
```

profile of v0, /device:TPU:1, one launch (start us, length us, event | category | flops | bytes accessed | tf_op | source)
XLA Modules:
  0.0 1293.6 jit_solution(11738205178397126315)
XLA Ops:
  10.7 9.3 all-to-all-start.4
  89.2 9.1 all-to-all-done.9
  144.8 8.3 all-to-all-done.11
  188.9 8.4 all-to-all-done.14
  231.7 7.3 all-to-all-done.16
  245.4 9.6 all-to-all-done.17
  263.8 7.9 all-to-all-done.18
  283.9 12.2 all_to_all.876
  457.0 7.4 all-to-all-done.34
  516.8 10.7 fusion.14
  540.9 8.3 all-to-all-done.26
  557.4 8.5 all-to-all-done.25
  635.3 7.5 all-to-all-done.38
  651.9 7.5 all-to-all-done.28
  693.9 12.0 all_to_all.877
  835.4 8.3 fusion.12
  874.4 7.4 all-to-all-start.57
  958.3 9.3 all-to-all-done.45
  998.8 8.4 all-to-all-done.47
  1015.1 27.4 %all-reduce.2 = (bf16[8,512]{1,0:T(8,128)(2,1)}, bf16[8,512]{1,0:T(8,128)(2,1)}) all-reduce(bf16[8,512]{1,0:T(8,128)(2,1)S(1)} %bitcast.1449, bf16[8,512]{1,0:T(8,128)(2,1)S(1)} %bitcast.1448), channel_id=1, replica_groups=mesh['dp'=8,'seq'=16] {'dp'}, use_global_device_ids=true, to_apply=%region_12.13 | all-reduce | flops 8192 | bytes 32768 | tf_op jit(solution)/shard_map/psum | solution.py:324
  1046.1 14.8 %all-to-all-start.49 = ((f32[1,16,32,128]{3,2,0,1:T(8,128)}), f32[1,16,32,128]{3,2,0,1:T(8,128)S(1)}, u32[]{:S(2)}, u32[]{:S(2)}) async-start(f32[1,16,32,128]{3,2,0,1:T(8,128)} %copy.829), calls=%async_computation.49 | async-start | bytes 524288 | tf_op jit(solution)/shard_map/all_to_all | solution.py:163
  1062.2 7.4 all-to-all-done.49
  1075.5 66.5 %all-reduce = (f32[3,384]{1,0:T(4,128)S(1)}, f32[128]{0:T(128)S(1)}, f32[128]{0:T(128)S(1)}) all-reduce(f32[3,384]{1,0:T(4,128)S(1)} %pad_maximum_fusion.3, f32[128]{0:T(128)S(1)} %copy-done.70, f32[128]{0:T(128)S(1)} %copy-done.69), channel_id=1, replica_groups=mesh['dp'=8,'seq'=16] {'dp','seq'}, use_global_device_ids=true, to_apply=%region_5.6 | all-reduce | flops 1408 | bytes 11264 | tf_op jit(solution)/shard_map/psum | solution.py:320
  1145.6 137.8 %all-reduce.5.cloned.1.call-done = (f32[128,384]{0,1:T(8,128)}, f32[128,128]{1,0:T(8,128)}) async-done(((f32[128,384]{0,1:T(8,128)}, f32[128,128]{1,0:T(8,128)}), (f32[128,384]{0,1:T(8,128)}, f32[128,128]{1,0:T(8,128)})) %all-reduce.5.cloned.1.call-update) | async-done | bytes 262160 | tf_op jit(solution)/shard_map/psum | solution.py:320
  (628 shorter events, 855.7 us)
Async XLA Ops:
  10.7 17.3 %all-to-all-start.4 = ((f32[16,1,256]{2,1,0:T(1,128)}), f32[16,1,256]{2,1,0:T(1,128)S(1)}, u32[]{:S(2)}, u32[]{:S(2)}) async-start(f32[16,1,256]{2,1,0:T(1,128)} %reshape.1187), calls=%async_computation.4 | async-start | bytes 32768 | tf_op jit(solution)/shard_map/all_to_all | solution.py:150
  21.2 27.8 %collective-permute-start = (f32[1,1,2,384]{3,2,1,0:T(2,128)S(1)}, f32[1,1,2,384]{3,2,1,0:T(2,128)S(1)}, u32[]{:S(2)}, u32[]{:S(2)}) collective-permute-start(f32[1,1,2,384]{3,2,1,0:T(2,128)S(1)} %slice.53), channel_id=1, source_target_pairs={{0,1},{1,2},{2,3},{3,4},{4,5},{5,6},{6,7},{7,8},{8,9},{9,10},{10,1... | collective-permute-start | bytes 9224 | tf_op jit(solution)/shard_map/ppermute | solution.py:13
  222.0 17.0 %all-to-all-start.16 = ((f32[1,2,512,128]{3,1,0,2:T(2,128)}), f32[1,2,512,128]{3,1,0,2:T(2,128)}, u32[]{:S(2)}, u32[]{:S(2)}) async-start(f32[1,2,512,128]{3,1,0,2:T(2,128)} %copy.682), calls=%async_computation.16 | async-start | bytes 1048576 | tf_op jit(solution)/shard_map/all_to_all | solution.py:159
  296.1 19.9 %all-to-all-start.30 = ((f32[1,1,512,128]{3,1,0,2:T(1,128)}), f32[1,1,512,128]{3,1,0,2:T(1,128)}, u32[]{:S(2)}, u32[]{:S(2)}) async-start(f32[1,1,512,128]{3,1,0,2:T(1,128)} %bitcast.259), calls=%async_computation.30 | async-start | bytes 524288 | tf_op jit(solution)/shard_map/all_to_all | solution.py:150
  330.7 17.8 %all-to-all-start.31 = ((f32[1,32,32,128]{3,2,0,1:T(8,128)}), f32[1,32,32,128]{3,2,0,1:T(8,128)}, u32[]{:S(2)}, u32[]{:S(2)}) async-start(f32[1,32,32,128]{3,2,0,1:T(8,128)} %copy.745), calls=%async_computation.31 | async-start | bytes 1048576 | tf_op jit(solution)/shard_map/all_to_all | solution.py:142
  348.5 19.5 %all-to-all-start.32 = ((f32[1,32,32,128]{3,2,0,1:T(8,128)}), f32[1,32,32,128]{3,2,0,1:T(8,128)}, u32[]{:S(2)}, u32[]{:S(2)}) async-start(f32[1,32,32,128]{3,2,0,1:T(8,128)} %copy.748), calls=%async_computation.32 | async-start | bytes 1048576 | tf_op jit(solution)/shard_map/all_to_all | solution.py:143
  368.1 18.7 %all-to-all-start.21 = ((f32[1,32,32,128]{3,2,0,1:T(8,128)}), f32[1,32,32,128]{3,2,0,1:T(8,128)}, u32[]{:S(2)}, u32[]{:S(2)}) async-start(f32[1,32,32,128]{3,2,0,1:T(8,128)} %copy.700), calls=%async_computation.21 | async-start | bytes 1048576 | tf_op jit(solution)/shard_map/all_to_all | solution.py:143
  386.8 16.6 %all-to-all-start.20 = ((f32[1,32,32,128]{3,2,0,1:T(8,128)}), f32[1,32,32,128]{3,2,0,1:T(8,128)}, u32[]{:S(2)}, u32[]{:S(2)}) async-start(f32[1,32,32,128]{3,2,0,1:T(8,128)} %copy.697), calls=%async_computation.20 | async-start | bytes 1048576 | tf_op jit(solution)/shard_map/all_to_all | solution.py:142
  447.7 16.6 %all-to-all-start.34 = ((f32[1,2,512,128]{3,1,0,2:T(2,128)}), f32[1,2,512,128]{3,1,0,2:T(2,128)}, u32[]{:S(2)}, u32[]{:S(2)}) async-start(f32[1,2,512,128]{3,1,0,2:T(2,128)} %copy.763), calls=%async_computation.34 | async-start | bytes 1048576 | tf_op jit(solution)/shard_map/all_to_all | solution.py:173
  464.3 17.0 %all-to-all-start.24 = ((f32[1,2,512,128]{3,1,0,2:T(2,128)}), f32[1,2,512,128]{3,1,0,2:T(2,128)}, u32[]{:S(2)}, u32[]{:S(2)}) async-start(f32[1,2,512,128]{3,1,0,2:T(2,128)} %copy.719), calls=%async_computation.24 | async-start | bytes 1048576 | tf_op jit(solution)/shard_map/all_to_all | solution.py:173
  481.4 22.5 %all-to-all-start.22 = ((f32[1,2,512,128]{3,1,0,2:T(2,128)}), f32[1,2,512,128]{3,1,0,2:T(2,128)}, u32[]{:S(2)}, u32[]{:S(2)}) async-start(f32[1,2,512,128]{3,1,0,2:T(2,128)} %copy.708), calls=%async_computation.22 | async-start | bytes 1048576 | tf_op jit(solution)/shard_map/all_to_all | solution.py:172
  530.6 18.7 %all-to-all-start.26 = ((f32[1,32,32,128]{3,2,0,1:T(8,128)}), f32[1,32,32,128]{3,2,0,1:T(8,128)S(1)}, u32[]{:S(2)}, u32[]{:S(2)}) async-start(f32[1,32,32,128]{3,2,0,1:T(8,128)} %copy.725), calls=%async_computation.26 | async-start | bytes 1048576 | tf_op jit(solution)/shard_map/all_to_all | solution.py:183
  549.3 16.6 %all-to-all-start.25 = ((f32[1,32,32,128]{3,2,0,1:T(8,128)}), f32[1,32,32,128]{3,2,0,1:T(8,128)}, u32[]{:S(2)}, u32[]{:S(2)}) async-start(f32[1,32,32,128]{3,2,0,1:T(8,128)} %copy.723), calls=%async_computation.25 | async-start | bytes 1048576 | tf_op jit(solution)/shard_map/all_to_all | solution.py:182
  565.9 16.8 %all-to-all-start.36 = ((f32[1,32,32,128]{3,2,0,1:T(8,128)}), f32[1,32,32,128]{3,2,0,1:T(8,128)}, u32[]{:S(2)}, u32[]{:S(2)}) async-start(f32[1,32,32,128]{3,2,0,1:T(8,128)} %copy.769), calls=%async_computation.36 | async-start | bytes 1048576 | tf_op jit(solution)/shard_map/all_to_all | solution.py:183
  609.3 16.8 %all-to-all-start.37 = ((f32[1,2,512,128]{3,1,0,2:T(2,128)}), f32[1,2,512,128]{3,1,0,2:T(2,128)}, u32[]{:S(2)}, u32[]{:S(2)}) async-start(f32[1,2,512,128]{3,1,0,2:T(2,128)} %copy.774), calls=%async_computation.37 | async-start | bytes 1048576 | tf_op jit(solution)/shard_map/all_to_all | solution.py:159
  626.1 16.6 %all-to-all-start.38 = ((f32[1,2,512,128]{3,1,0,2:T(2,128)}), f32[1,2,512,128]{3,1,0,2:T(2,128)}, u32[]{:S(2)}, u32[]{:S(2)}) async-start(f32[1,2,512,128]{3,1,0,2:T(2,128)} %copy.780), calls=%async_computation.38 | async-start | bytes 1048576 | tf_op jit(solution)/shard_map/all_to_all | solution.py:160
  642.7 16.6 %all-to-all-start.28 = ((f32[1,2,512,128]{3,1,0,2:T(2,128)}), f32[1,2,512,128]{3,1,0,2:T(2,128)}, u32[]{:S(2)}, u32[]{:S(2)}) async-start(f32[1,2,512,128]{3,1,0,2:T(2,128)} %copy.736), calls=%async_computation.28 | async-start | bytes 1048576 | tf_op jit(solution)/shard_map/all_to_all | solution.py:160
  708.8 17.2 %all-to-all-start.40 = ((f32[1,1,512,128]{3,1,0,2:T(1,128)}), f32[1,1,512,128]{3,1,0,2:T(1,128)}, u32[]{:S(2)}, u32[]{:S(2)}) async-start(f32[1,1,512,128]{3,1,0,2:T(1,128)} %bitcast.1339), calls=%async_computation.40 | async-start | bytes 524288 | tf_op jit(solution)/shard_map/all_to_all | solution.py:150
  792.6 18.3 %all-to-all-start.43 = ((f32[1,2,512,128]{3,1,0,2:T(2,128)}), f32[1,2,512,128]{3,1,0,2:T(2,128)}, u32[]{:S(2)}, u32[]{:S(2)}) async-start(f32[1,2,512,128]{3,1,0,2:T(2,128)} %copy.800), calls=%async_computation.43 | async-start | bytes 1048576 | tf_op jit(solution)/shard_map/all_to_all | solution.py:172
  911.1 21.9 %all-to-all-start.52 = ((f32[16,1,512]{2,1,0:T(1,128)}), f32[16,1,512]{2,1,0:T(1,128)}, u32[]{:S(2)}, u32[]{:S(2)}) async-start(f32[16,1,512]{2,1,0:T(1,128)} %reshape.1213), calls=%async_computation.52 | async-start | bytes 65536 | tf_op jit(solution)/shard_map/all_to_all | solution.py:159
  933.1 18.7 %all-to-all-start.46 = ((f32[1,32,32,128]{3,2,0,1:T(8,128)}), f32[1,32,32,128]{3,2,0,1:T(8,128)S(1)}, u32[]{:S(2)}, u32[]{:S(2)}) async-start(f32[1,32,32,128]{3,2,0,1:T(8,128)} %copy.813), calls=%async_computation.46 | async-start | bytes 1048576 | tf_op jit(solution)/shard_map/all_to_all | solution.py:183
  1007.2 35.4 %all-to-all-start.48 = ((f32[1,2,512,128]{3,1,0,2:T(2,128)}), f32[1,2,512,128]{3,1,0,2:T(2,128)S(1)}, u32[]{:S(2)}, u32[]{:S(2)}) async-start(f32[1,2,512,128]{3,1,0,2:T(2,128)} %copy.824), calls=%async_computation.48 | async-start | bytes 1048576 | tf_op jit(solution)/shard_map/all_to_all | solution.py:160
  1046.1 23.5 %all-to-all-start.49 = ((f32[1,16,32,128]{3,2,0,1:T(8,128)}), f32[1,16,32,128]{3,2,0,1:T(8,128)S(1)}, u32[]{:S(2)}, u32[]{:S(2)}) async-start(f32[1,16,32,128]{3,2,0,1:T(8,128)} %copy.829), calls=%async_computation.49 | async-start | bytes 524288 | tf_op jit(solution)/shard_map/all_to_all | solution.py:163
  1060.9 222.4 %all-reduce.5.cloned.1.call-start = ((), (), s32[]{:S(2)}) async-start(), calls=%async_computation.60 | async-start | bytes 524288 | tf_op jit(solution)/shard_map/psum | solution.py:320
  (108 other events, 1326.8 us)
Sparse Core Ops, SparseCore 0:
  1144.8 138.5 all-reduce.4
where the time goes:
time: 1310 us; the launch traced here: 1290 us
  waiting for transfers between devices  427 us (33%)
  starting transfers between devices  315 us (24%)
  local copies, waits for them, and re-layouts  193 us (15%)
  matrix products  149 us (11%)
  blocking collectives  118 us (9%)
  other arithmetic  75 us (6%)
  between operations  16.5 us (1%)
    psum x1, waiting for transfers between devices, shards(): lax.psum((local_w_in, local_w_out, local_taps, local_skip_one, local_skip...  138 us
    psum x1, blocking collectives, shards(): lax.psum((local_w_in, local_w_out, local_taps, local_skip_one, local_skip...  66.5 us
    unnamed x186, local copies, waits for them, and re-layouts  50.7 us
    all_to_all x6, waiting for transfers between devices, restore_spectrum(): lax.all_to_all(real_part, 'seq', split_axis=1, concat_axis=2, tiled=True)  38.3 us
    all_to_all x6, starting transfers between devices, restore_spectrum(): lax.all_to_all(imag_part, 'seq', split_axis=1, concat_axis=2, tiled=True)  37.1 us
    all_to_all x6, waiting for transfers between devices, signal(): lax.all_to_all(imag_part, 'seq', split_axis=2, concat_axis=1, tiled=True)  34.4 us
    all_to_all x5, starting transfers between devices, signal(): lax.all_to_all(columns, 'seq', split_axis=1, concat_axis=2, tiled=True)  34.3 us
    all_to_all x6, waiting for transfers between devices, order_spectrum(): lax.all_to_all(imag_part, 'seq', split_axis=2, concat_axis=1, tiled=True)  33.6 us
  transfers between devices with their start and end apart: 61, of which 52 were waited for; matrix products, arithmetic and copies ran while one was open for 23% of the time, Pallas kernels for 0%

commit v1 on v0

--- a/solution.py
+++ b/solution.py
@@ -5,6 +5,14 @@
 from jax.sharding import PartitionSpec as P
 
 FACTOR = 32
+
+
+def define_leaf_here(array_dim, in_dim, x0):
+    z = jnp.concatenate(
+        lax.all_to_all(jnp.stack(jnp.split(x0, lax.axis_size("seq"), array_dim), 0), "seq", 0, 0),
+        in_dim,
+    )
+    return z
 
 
 def passed_along(block, axis, distance):
@@ -140,7 +148,7 @@
     return local_dft(
         (
             lax.all_to_all(real_part, "seq", split_axis=1, concat_axis=2, tiled=True),
-            lax.all_to_all(imag_part, "seq", split_axis=1, concat_axis=2, tiled=True),
+            define_leaf_here(1, 2, x0=imag_part),
         )
     )
 

time: 1310 us -> 1350 us (1.031)
  local copies, waits for them, and re-layouts: 193 us -> 239 us
  blocking collectives: 118 us -> 93.9 us
  starting transfers between devices: 315 us -> 336 us
    unnamed x186 -> x280, local copies, waits for them, and re-layouts: 50.7 us -> 96.3 us
    all_to_all x2 -> x0, blocking collectives: 24.2 us -> none  [the longest x1 12.2 us: spectrum(): lax.all_to_all(field, 'seq', split_axis=2, concat_axis=1, tiled=True)]
    all_to_all x5 -> x6, starting transfers between devices: 34.3 us -> 39 us  [signal(): lax.all_to_all(columns, 'seq', split_axis=1, concat_axis=2, tiled=True)]
    all_to_all x5 -> x6, starting transfers between devices: 29.4 us -> 33.6 us  [spectrum(): lax.all_to_all(field, 'seq', split_axis=2, concat_axis=1, tiled=True)]
    all_to_all x5 -> x6, waiting for transfers between devices: 28.9 us -> 32.2 us  [signal(): lax.all_to_all(columns, 'seq', split_axis=1, concat_axis=2, tiled=True)]
  transfers between devices with their start and end apart: 61 -> 63, of which waited for: 52 -> 50; matrix products, arithmetic and copies ran while one was open for 23% -> 27% of each run, Pallas kernels for 0% -> 0%
where the time goes in v1:
time: 1350 us; the launch traced here: 1330 us
  waiting for transfers between devices  414 us (31%)
  starting transfers between devices  336 us (25%)
  local copies, waits for them, and re-layouts  239 us (18%)
  matrix products  156 us (12%)
  blocking collectives  93.9 us (7%)
  other arithmetic  75.1 us (6%)
  between operations  16.8 us (1%)
    psum x1, waiting for transfers between devices, shards(): lax.psum((local_w_in, local_w_out, local_taps, local_skip_one, local_skip...  138 us
    unnamed x280, local copies, waits for them, and re-layouts  96.3 us
    psum x1, blocking collectives, shards(): lax.psum((local_w_in, local_w_out, local_taps, local_skip_one, local_skip...  66.5 us
    all_to_all x6, starting transfers between devices, signal(): lax.all_to_all(columns, 'seq', split_axis=1, concat_axis=2, tiled=True)  39 us
    all_to_all x6, waiting for transfers between devices, order_spectrum(): lax.all_to_all(imag_part, 'seq', split_axis=2, concat_axis=1, tiled=True)  38.8 us
    all_to_all x6, waiting for transfers between devices, restore_spectrum(): lax.all_to_all(real_part, 'seq', split_axis=1, concat_axis=2, tiled=True)  35.8 us
    all_to_all x6, starting transfers between devices, to_frequency(): lax.all_to_all(real_part, 'seq', split_axis=1, concat_axis=2, tiled=True)  35.8 us
    all_to_all x6, starting transfers between devices, restore_spectrum(): lax.all_to_all(imag_part, 'seq', split_axis=1, concat_axis=2, tiled=True)  34.5 us
  transfers between devices with their start and end apart: 63, of which 50 were waited for; matrix products, arithmetic and copies ran while one was open for 27% of the time, Pallas kernels for 0%

profile of v1, /device:TPU:1, one launch (start us, length us, event | category | flops | bytes accessed | tf_op | source)
XLA Modules:
  0.0 1330.5 jit_solution(12660615146421666511)
XLA Ops:
  10.7 9.3 all-to-all-start.4
  148.2 8.3 all-to-all-done.11
  161.7 10.7 all-to-all-done.13
  195.9 7.3 all-to-all-start.14
  206.2 8.3 all-to-all-done.14
  247.1 7.8 all-to-all-start.16
  397.8 9.6 all-to-all-done.20
  454.5 7.3 all-to-all-start.23
  494.4 7.4 all-to-all-done.34
  554.2 10.7 fusion.14
  578.3 8.3 all-to-all-done.26
  594.7 8.5 all-to-all-done.25
  672.7 7.5 all-to-all-done.38
  689.3 7.4 all-to-all-done.28
  872.2 8.3 fusion.12
  911.1 7.4 all-to-all-start.57
  969.8 7.3 all-to-all-start.46
  995.1 9.3 all-to-all-done.45
  1035.6 8.4 all-to-all-done.47
  1051.9 27.3 %all-reduce.2 = (bf16[8,512]{1,0:T(8,128)(2,1)}, bf16[8,512]{1,0:T(8,128)(2,1)}) all-reduce(bf16[8,512]{1,0:T(8,128)(2,1)S(1)} %bitcast.1811, bf16[8,512]{1,0:T(8,128)(2,1)S(1)} %bitcast.1810), channel_id=1, replica_groups=mesh['dp'=8,'seq'=16] {'dp'}, use_global_device_ids=true, to_apply=%region_12.13 | all-reduce | flops 8192 | bytes 32768 | tf_op jit(solution)/shard_map/psum | solution.py:332
  1082.9 14.8 %all-to-all-start.49 = ((f32[1,16,32,128]{3,2,0,1:T(8,128)}), f32[1,16,32,128]{3,2,0,1:T(8,128)S(1)}, u32[]{:S(2)}, u32[]{:S(2)}) async-start(f32[1,16,32,128]{3,2,0,1:T(8,128)} %copy.813), calls=%async_computation.49 | async-start | bytes 524288 | tf_op jit(solution)/shard_map/all_to_all | solution.py:171
  1099.0 7.4 all-to-all-done.49
  1112.3 66.5 %all-reduce = (f32[3,384]{1,0:T(4,128)S(1)}, f32[128]{0:T(128)S(1)}, f32[128]{0:T(128)S(1)}) all-reduce(f32[3,384]{1,0:T(4,128)S(1)} %pad_maximum_fusion.3, f32[128]{0:T(128)S(1)} %copy-done.72, f32[128]{0:T(128)S(1)} %copy-done.71), channel_id=1, replica_groups=mesh['dp'=8,'seq'=16] {'dp','seq'}, use_global_device_ids=true, to_apply=%region_5.6 | all-reduce | flops 1408 | bytes 11264 | tf_op jit(solution)/shard_map/psum | solution.py:328
  1182.4 137.8 %all-reduce.5.cloned.1.call-done = (f32[128,384]{0,1:T(8,128)}, f32[128,128]{1,0:T(8,128)}) async-done(((f32[128,384]{0,1:T(8,128)}, f32[128,128]{1,0:T(8,128)}), (f32[128,384]{0,1:T(8,128)}, f32[128,128]{1,0:T(8,128)})) %all-reduce.5.cloned.1.call-update) | async-done | bytes 262160 | tf_op jit(solution)/shard_map/psum | solution.py:328
  (721 shorter events, 900.6 us)
Async XLA Ops:
  10.7 19.5 %all-to-all-start.4 = ((f32[16,1,256]{2,1,0:T(1,128)}), f32[16,1,256]{2,1,0:T(1,128)S(1)}, u32[]{:S(2)}, u32[]{:S(2)}) async-start(f32[16,1,256]{2,1,0:T(1,128)} %reshape.1199), calls=%async_computation.4 | async-start | bytes 32768 | tf_op jit(solution)/shard_map/all_to_all | solution.py:158
  100.5 17.3 %all-to-all-start.10 = ((f32[16,1,2,32,128]{4,2,3,1,0:T(2,128)}), f32[16,1,2,32,128]{4,2,3,1,0:T(2,128)S(1)}, u32[]{:S(2)}, u32[]{:S(2)}) async-start(f32[16,1,2,32,128]{4,2,3,1,0:T(2,128)} %constant_dynamic-update-slice_fusion.32), calls=%async_computation.10 | async-start | bytes 1048576 | tf_op jit(solution)/shard_map/all_to_all | solution.py:12
  172.4 23.5 %all-to-all-start.2 = ((f32[16,1,512]{2,1,0:T(1,128)}), f32[16,1,512]{2,1,0:T(1,128)}, u32[]{:S(2)}, u32[]{:S(2)}) async-start(f32[16,1,512]{2,1,0:T(1,128)} %reshape.1211), calls=%async_computation.2 | async-start | bytes 65536 | tf_op jit(solution)/shard_map/all_to_all | solution.py:12
  195.9 18.7 %all-to-all-start.14 = ((f32[1,32,32,128]{3,2,0,1:T(8,128)}), f32[1,32,32,128]{3,2,0,1:T(8,128)S(1)}, u32[]{:S(2)}, u32[]{:S(2)}) async-start(f32[1,32,32,128]{3,2,0,1:T(8,128)} %copy.663), calls=%async_computation.14 | async-start | bytes 1048576 | tf_op jit(solution)/shard_map/all_to_all | solution.py:190
  214.6 17.1 %all-to-all-start.15 = ((f32[1,32,32,128]{3,2,0,1:T(8,128)}), f32[1,32,32,128]{3,2,0,1:T(8,128)}, u32[]{:S(2)}, u32[]{:S(2)}) async-start(f32[1,32,32,128]{3,2,0,1:T(8,128)} %copy.665), calls=%async_computation.15 | async-start | bytes 1048576 | tf_op jit(solution)/shard_map/all_to_all | solution.py:191
  247.1 23.8 %all-to-all-start.16 = ((f32[1,2,512,128]{3,1,0,2:T(2,128)}), f32[1,2,512,128]{3,1,0,2:T(2,128)}, u32[]{:S(2)}, u32[]{:S(2)}) async-start(f32[1,2,512,128]{3,1,0,2:T(2,128)} %copy.672), calls=%async_computation.16 | async-start | bytes 1048576 | tf_op jit(solution)/shard_map/all_to_all | solution.py:167
  270.9 18.7 %all-to-all-start.17 = ((f32[1,2,512,128]{3,1,0,2:T(2,128)}), f32[1,2,512,128]{3,1,0,2:T(2,128)}, u32[]{:S(2)}, u32[]{:S(2)}) async-start(f32[1,2,512,128]{3,1,0,2:T(2,128)} %copy.678), calls=%async_computation.17 | async-start | bytes 1048576 | tf_op jit(solution)/shard_map/all_to_all | solution.py:168
  323.0 18.8 %all-to-all-start.30 = ((f32[1,1,512,128]{3,1,0,2:T(1,128)}), f32[1,1,512,128]{3,1,0,2:T(1,128)}, u32[]{:S(2)}, u32[]{:S(2)}) async-start(f32[1,1,512,128]{3,1,0,2:T(1,128)} %bitcast.1702), calls=%async_computation.30 | async-start | bytes 524288 | tf_op jit(solution)/shard_map/all_to_all | solution.py:158
  347.8 40.8 %all-to-all-start.31 = ((f32[1,32,32,128]{3,2,0,1:T(8,128)}), f32[1,32,32,128]{3,2,0,1:T(8,128)}, u32[]{:S(2)}, u32[]{:S(2)}) async-start(f32[1,32,32,128]{3,2,0,1:T(8,128)} %copy.733), calls=%async_computation.31 | async-start | bytes 1048576 | tf_op jit(solution)/shard_map/all_to_all | solution.py:150
  388.6 18.7 %all-to-all-start.20 = ((f32[1,32,32,128]{3,2,0,1:T(8,128)}), f32[1,32,32,128]{3,2,0,1:T(8,128)}, u32[]{:S(2)}, u32[]{:S(2)}) async-start(f32[1,32,32,128]{3,2,0,1:T(8,128)} %copy.687), calls=%async_computation.20 | async-start | bytes 1048576 | tf_op jit(solution)/shard_map/all_to_all | solution.py:150
  501.8 17.0 %all-to-all-start.24 = ((f32[1,2,512,128]{3,1,0,2:T(2,128)}), f32[1,2,512,128]{3,1,0,2:T(2,128)}, u32[]{:S(2)}, u32[]{:S(2)}) async-start(f32[1,2,512,128]{3,1,0,2:T(2,128)} %copy.707), calls=%async_computation.24 | async-start | bytes 1048576 | tf_op jit(solution)/shard_map/all_to_all | solution.py:181
  518.8 22.5 %all-to-all-start.22 = ((f32[1,2,512,128]{3,1,0,2:T(2,128)}), f32[1,2,512,128]{3,1,0,2:T(2,128)}, u32[]{:S(2)}, u32[]{:S(2)}) async-start(f32[1,2,512,128]{3,1,0,2:T(2,128)} %copy.696), calls=%async_computation.22 | async-start | bytes 1048576 | tf_op jit(solution)/shard_map/all_to_all | solution.py:180
  567.9 18.7 %all-to-all-start.26 = ((f32[1,32,32,128]{3,2,0,1:T(8,128)}), f32[1,32,32,128]{3,2,0,1:T(8,128)S(1)}, u32[]{:S(2)}, u32[]{:S(2)}) async-start(f32[1,32,32,128]{3,2,0,1:T(8,128)} %copy.713), calls=%async_computation.26 | async-start | bytes 1048576 | tf_op jit(solution)/shard_map/all_to_all | solution.py:191
  603.3 16.8 %all-to-all-start.36 = ((f32[1,32,32,128]{3,2,0,1:T(8,128)}), f32[1,32,32,128]{3,2,0,1:T(8,128)}, u32[]{:S(2)}, u32[]{:S(2)}) async-start(f32[1,32,32,128]{3,2,0,1:T(8,128)} %copy.755), calls=%async_computation.36 | async-start | bytes 1048576 | tf_op jit(solution)/shard_map/all_to_all | solution.py:191
  646.7 16.8 %all-to-all-start.37 = ((f32[1,2,512,128]{3,1,0,2:T(2,128)}), f32[1,2,512,128]{3,1,0,2:T(2,128)}, u32[]{:S(2)}, u32[]{:S(2)}) async-start(f32[1,2,512,128]{3,1,0,2:T(2,128)} %copy.760), calls=%async_computation.37 | async-start | bytes 1048576 | tf_op jit(solution)/shard_map/all_to_all | solution.py:167
  663.5 16.6 %all-to-all-start.38 = ((f32[1,2,512,128]{3,1,0,2:T(2,128)}), f32[1,2,512,128]{3,1,0,2:T(2,128)}, u32[]{:S(2)}, u32[]{:S(2)}) async-start(f32[1,2,512,128]{3,1,0,2:T(2,128)} %copy.766), calls=%async_computation.38 | async-start | bytes 1048576 | tf_op jit(solution)/shard_map/all_to_all | solution.py:168
  785.4 17.6 %all-to-all-start.41 = ((f32[1,32,32,128]{3,2,0,1:T(8,128)}), f32[1,32,32,128]{3,2,0,1:T(8,128)}, u32[]{:S(2)}, u32[]{:S(2)}) async-start(f32[1,32,32,128]{3,2,0,1:T(8,128)} %copy.775), calls=%async_computation.41 | async-start | bytes 1048576 | tf_op jit(solution)/shard_map/all_to_all | solution.py:150
  802.9 16.6 %all-to-all-start.42 = ((f32[16,1,2,32,128]{4,2,3,1,0:T(2,128)}), f32[16,1,2,32,128]{4,2,3,1,0:T(2,128)}, u32[]{:S(2)}, u32[]{:S(2)}) async-start(f32[16,1,2,32,128]{4,2,3,1,0:T(2,128)} %constant_dynamic-update-slice_fusion.80), calls=%async_computation.42 | async-start | bytes 1048576 | tf_op jit(solution)/shard_map/all_to_all | solution.py:12
  829.6 18.0 %all-to-all-start.43 = ((f32[1,2,512,128]{3,1,0,2:T(2,128)}), f32[1,2,512,128]{3,1,0,2:T(2,128)}, u32[]{:S(2)}, u32[]{:S(2)}) async-start(f32[1,2,512,128]{3,1,0,2:T(2,128)} %copy.784), calls=%async_computation.43 | async-start | bytes 1048576 | tf_op jit(solution)/shard_map/all_to_all | solution.py:180
  947.9 22.0 %all-to-all-start.52 = ((f32[16,1,512]{2,1,0:T(1,128)}), f32[16,1,512]{2,1,0:T(1,128)}, u32[]{:S(2)}, u32[]{:S(2)}) async-start(f32[16,1,512]{2,1,0:T(1,128)} %reshape.1225), calls=%async_computation.52 | async-start | bytes 65536 | tf_op jit(solution)/shard_map/all_to_all | solution.py:167
  969.8 18.7 %all-to-all-start.46 = ((f32[1,32,32,128]{3,2,0,1:T(8,128)}), f32[1,32,32,128]{3,2,0,1:T(8,128)S(1)}, u32[]{:S(2)}, u32[]{:S(2)}) async-start(f32[1,32,32,128]{3,2,0,1:T(8,128)} %copy.797), calls=%async_computation.46 | async-start | bytes 1048576 | tf_op jit(solution)/shard_map/all_to_all | solution.py:191
  1044.0 35.3 %all-to-all-start.48 = ((f32[1,2,512,128]{3,1,0,2:T(2,128)}), f32[1,2,512,128]{3,1,0,2:T(2,128)S(1)}, u32[]{:S(2)}, u32[]{:S(2)}) async-start(f32[1,2,512,128]{3,1,0,2:T(2,128)} %copy.808), calls=%async_computation.48 | async-start | bytes 1048576 | tf_op jit(solution)/shard_map/all_to_all | solution.py:168
  1082.9 23.5 %all-to-all-start.49 = ((f32[1,16,32,128]{3,2,0,1:T(8,128)}), f32[1,16,32,128]{3,2,0,1:T(8,128)S(1)}, u32[]{:S(2)}, u32[]{:S(2)}) async-start(f32[1,16,32,128]{3,2,0,1:T(8,128)} %copy.813), calls=%async_computation.49 | async-start | bytes 524288 | tf_op jit(solution)/shard_map/all_to_all | solution.py:171
  1097.7 222.5 %all-reduce.5.cloned.1.call-start = ((), (), s32[]{:S(2)}) async-start(), calls=%async_computation.60 | async-start | bytes 524288 | tf_op jit(solution)/shard_map/psum | solution.py:328
  (112 other events, 1206.9 us)
Sparse Core Ops, SparseCore 0:
  1181.6 138.5 all-reduce.4
